TPU v7x, 32 devices: a whole 2x2x4 slice. The times are simulated.
32 devices in a mesh: groups: 2 (over x), corpus: 16 (over z, y, core).
Axes of the slice: x: 2, y: 2, z: 4, core: 2. Of those that a mesh axis runs over, the one named last changes fastest.
Arguments:
- queries: bfloat16 [1792, 32, 128], P(('groups', 'corpus')), parts along dimension 0, may hold values from -6 to 6
- passages: bfloat16 [4096, 128, 128], P(('groups', 'corpus')), parts along dimension 0, may hold values from -0.5 to 0.5
- lengths: int32 [4096], P(('groups', 'corpus')), parts along dimension 0, may hold values from 8 to 128
- candidates: int32 [32, 128], P(('groups', 'corpus')), parts along dimension 0, may hold values from 0 to 2047, as said below
Outputs:
- scores: float32 [1792, 128], P(('groups', 'corpus')), parts along dimension 0
- best_scores: float32 [1792, 100], P(('groups', 'corpus')), parts along dimension 0
There are 2 independent parts, one for each index of `groups`. A program takes and returns all parts, laid end to end along the dimension named above; each array names one. Nothing has to cross between parts.
Inputs may be any that keep to these rules, and one draw needn't show every extreme that they name: Row b lists the candidates of queries b * 56 to (b + 1) * 56 - 1. Passage p is held by owner p // 128. In every row at most 12 entries share an owner, and in every row some owner holds exactly 12 of them. Entries may repeat. `lengths`: rows of a tile at or past its length are padding.
All inputs are finite; a program needn't handle non-finite values.
Results may differ from a plain program's by a relative error of at most 0.0003.
Values may be sent and summed in bfloat16 or wider, within the bound.
A program may use at most 128 MiB of HBM per device.

v0:
```python
import math
import jax
import jax.numpy as jnp
from jax import lax
from jax.sharding import PartitionSpec as P

TOPK = 100


def maxsim_many(query_sets, tile_sets, per_device):
    similar = jnp.einsum(
        "srd,sgpd->srgp", query_sets, tile_sets, preferred_element_type=jnp.float32
    )
    nearest = jnp.max(similar, axis=3)
    shards_now = query_sets.shape[0]
    query_tok = query_sets.shape[1] // per_device
    return jnp.sum(
        nearest.reshape(shards_now, per_device, query_tok, nearest.shape[2]), axis=2
    ) / float(query_tok)


def fill_rows(tile_set, tile_len):
    inside = lax.broadcasted_iota(jnp.int32, tile_set.shape[:2], 1) < tile_len[:, None]
    return jnp.where(inside[:, :, None], tile_set, tile_set[:, :1, :])


def local(queries, passages, lengths, candidates):
    peers = lax.axis_size("corpus")
    per_owner, tile_rows, feature = passages.shape
    per_device, query_tok = (queries.shape[0], queries.shape[1])
    candidate_ids = candidates[0]
    number = candidate_ids.shape[0]
    capacity = max(2, 3 * number // (2 * peers))
    owner_of = candidate_ids // per_owner
    local_id = candidate_ids - owner_of * per_owner
    position = jnp.arange(number, dtype=jnp.int32)
    shared = (owner_of[:, None] == owner_of[None, :]) & (position[None, :] < position[:, None])
    rank_in = jnp.sum(shared.astype(jnp.int32), axis=1)
    slot_of = owner_of * capacity + rank_in
    matches = slot_of[None, :] == jnp.arange(peers * capacity, dtype=jnp.int32)[:, None]
    wanted = jnp.max(jnp.where(matches, local_id[None, :], -1), axis=1).reshape(peers, capacity)
    asked = lax.all_to_all(wanted, "corpus", split_axis=0, concat_axis=0, tiled=True)
    picked = jnp.maximum(asked.reshape(-1), 0)
    chosen = fill_rows(passages[picked], lengths[picked])
    by_scorer = chosen.reshape(peers, capacity, tile_rows, feature)
    stacked = queries.reshape(1, per_device * query_tok, feature)
    piece = lax.all_gather(stacked, "corpus", axis=0, tiled=True)
    shards_here = piece.shape[0]
    group_size = math.gcd(shards_here, 8)
    turns = shards_here // group_size
    query_groups = piece.reshape(turns, group_size, piece.shape[1], feature)
    tile_groups = by_scorer.reshape(turns, group_size, capacity, tile_rows, feature)
    fresh_scores = lax.map(
        lambda paired: maxsim_many(paired[0], paired[1], per_device), (query_groups, tile_groups)
    )
    fresh_scores = fresh_scores.reshape(shards_here, per_device, capacity)
    returned = lax.all_to_all(fresh_scores, "corpus", split_axis=0, concat_axis=0, tiled=True)
    spread = jnp.transpose(returned, (1, 0, 2)).reshape(per_device, peers * capacity)
    scores = jnp.take(spread, slot_of, axis=1)
    best_scores = lax.top_k(scores, TOPK)[0]
    return (scores, best_scores)


def solution(mesh):
    return jax.shard_map(
        local,
        mesh=mesh,
        in_specs=(
            P(("groups", "corpus"), None, None),
            P(("groups", "corpus"), None, None),
            P(("groups", "corpus")),
            P(("groups", "corpus"), None),
        ),
        out_specs=(P(("groups", "corpus"), None), P(("groups", "corpus"), None)),
        check_vma=False,
    )
```

profile of v0, /device:TPU:0, one launch (start us, length us, event | category | flops | bytes accessed | tf_op | source)
XLA Modules:
  0.0 137.0 jit_solution(5977993929277204286)
XLA Ops:
  7.2 0.0 copy-start
  7.2 0.0 all-gather.2.cloned.1.call-start
  7.2 0.7 all-gather.2.cloned.1.call-update
  7.9 0.7 subtract_bitcast_fusion
  8.6 0.7 and_select_fusion.2
  9.2 0.2 convert_reduce_fusion
  9.4 0.1 select_reduce_fusion
  9.6 0.7 all_to_all.9
  10.3 7.4 %all-to-all-start = ((s32[16,1,12]{2,1,0:T(1,128)}), s32[16,1,12]{2,1,0:T(1,128)S(1)}, u32[]{:S(2)}, u32[]{:S(2)}) async-start(s32[16,1,12]{2,1,0:T(1,128)} %bitcast.12), calls=%async_computation | async-start | bytes 16384 | tf_op jit(solution)/shard_map/all_to_all | solution.py:42
  17.7 0.7 fusion.6
  18.3 0.7 compare_and_fusion
  19.0 5.0 %all-to-all-done = s32[16,1,12]{2,1,0:T(1,128)S(1)} async-done(((s32[16,1,12]{2,1,0:T(1,128)}), s32[16,1,12]{2,1,0:T(1,128)S(1)}, u32[]{:S(2)}, u32[]{:S(2)}) %all-to-all-start) | async-done | bytes 800 | tf_op jit(solution)/shard_map/all_to_all | solution.py:42
  24.1 0.1 reshape.184
  24.2 10.2 %gather_fusion.1 = bf16[192,128,128]{2,1,0:T(8,128)(2,1)} fusion(bf16[128,128,128]{2,1,0:T(8,128)(2,1)} %param.7, s32[1024]{0:T(1024)S(1)} %pad_clamp_fusion.1), kind=kCustom, calls=%fused_computation.1 | custom fusion | bytes 12583680 | tf_op jit(solution)/shard_map/gather | solution.py:44
  34.3 1.3 slice_reduce_fusion
  35.6 0.0 copy-done
  35.6 1.6 %gather_fusion = s32[192]{0:T(256)S(1)} fusion(s32[128]{0:T(128)S(1)} %copy-done, s32[1024]{0:T(1024)S(1)} %pad_clamp_fusion.1), kind=kCustom, calls=%fused_computation | custom fusion | bytes 2304 | tf_op jit(solution)/shard_map/gather | solution.py:44
  37.2 0.1 lt.53
  37.3 0.1 iota_compare_fusion
  37.4 6.5 %broadcast_select_fusion = bf16[2,8,12,128,128]{4,3,2,1,0:T(8,128)(2,1)} fusion(bf16[2,8,12,128,128]{4,3,2,1,0:T(8,128)(2,1)} %bitcast.73, pred[2,8,12,128]{3,2,1,0:T(8,128)(4,1)S(1)} %iota_compare_fusion, bf16[2,8,12,128]{3,2,1,0:T(8,128)(2,1)S(1)} %broadcast_in_dim.64), kind=kLoop, calls=%fused_computation.10 | loop fusion | flops 3145728 | bytes 12656640 | tf_op jit(solution)/shard_map/jit(_where)/select_n | solution.py:24
  43.9 36.8 %all-gather.2.cloned.1.call-done = bf16[16,1792,128]{2,1,0:T(8,128)(2,1)} async-done(((bf16[1,1792,128]{2,1,0:T(8,128)(2,1)}), bf16[16,1792,128]{2,1,0:T(8,128)(2,1)}) %all-gather.2.cloned.1.call-update) | async-done | bytes 7340048 | tf_op jit(solution)/shard_map/all_gather | solution.py:47
  80.7 32.9 %while.10 = (s32[]{:T(128)}, f32[2,8,56,12]{2,1,0,3:T(8,128)S(1)}, bf16[2,8,1792,128]{3,2,1,0:T(8,128)(2,1)}, bf16[2,8,12,128,128]{4,3,2,1,0:T(8,128)(2,1)}, s32[]{:T(128)}, /*index=5*/f32[]{:T(128)}) while((s32[]{:T(128)}, f32[2,8,56,12]{2,1,0,3:T(8,128)S(1)}, bf16[2,8,1792,128]{3,2,1,0:T(8,128)(2,1)}, ...), condition=%wide.region_5.6_spmd, body=%wide.region_2.5_spmd.sunk | while | flops 5659164672 | bytes 11065421 | solution.py:53
  80.7 14.4 %convolution_reduce_fusion.2 = f32[8,1792,12]{1,2,0:T(8,128)S(1)} fusion(bf16[2,8,1792,128]{3,2,1,0:T(8,128)(2,1)} %get-tuple-element.87, s32[]{:T(128)} %get-tuple-element.79, bf16[2,8,12,128,128]{4,3,2,1,0:T(8,128)(2,1)} %get-tuple-element.88), kind=kOutput, calls=%fused_computation.3.clone.1 | convolution fusion | flops 5658992640 | bytes 7504896 | tf_op jit(solution)/shard_map/while/body/eval_jaxpr/srd,sgpd->srgp/dot_general | solution.py:11
  95.1 0.4 copy.35
  95.5 0.8 reshape.220
  96.4 0.8 reduce_sum.27
  97.2 14.4 %convolution_reduce_fusion.2 = f32[8,1792,12]{1,2,0:T(8,128)S(1)} fusion(bf16[2,8,1792,128]{3,2,1,0:T(8,128)(2,1)} %get-tuple-element.87, s32[]{:T(128)} %get-tuple-element.79, bf16[2,8,12,128,128]{4,3,2,1,0:T(8,128)(2,1)} %get-tuple-element.88), kind=kOutput, calls=%fused_computation.3.clone.1 | convolution fusion | flops 5658992640 | bytes 7504896 | tf_op jit(solution)/shard_map/while/body/eval_jaxpr/srd,sgpd->srgp/dot_general | solution.py:11
  111.6 0.4 copy.35
  112.0 0.8 reshape.220
  112.8 0.8 reduce_sum.27
  113.7 0.8 reshape.217
  114.5 3.5 %all-to-all-start.1 = ((f32[16,1,672]{2,1,0:T(1,128)}), f32[16,1,672]{2,1,0:T(1,128)S(1)}, u32[]{:S(2)}, u32[]{:S(2)}) async-start(f32[16,1,672]{2,1,0:T(1,128)} %reshape.217), calls=%async_computation.1 | async-start | bytes 98304 | tf_op jit(solution)/shard_map/all_to_all | solution.py:57
  118.0 6.7 %all-to-all-done.1 = f32[16,1,672]{2,1,0:T(1,128)S(1)} async-done(((f32[16,1,672]{2,1,0:T(1,128)}), f32[16,1,672]{2,1,0:T(1,128)S(1)}, u32[]{:S(2)}, u32[]{:S(2)}) %all-to-all-start.1) | async-done | bytes 43040 | tf_op jit(solution)/shard_map/all_to_all | solution.py:57
  124.7 0.5 broadcast.219
  125.2 0.8 reduce.6
  126.0 0.1 reshape.218
  126.1 0.6 gather_fusion.2
  126.8 0.1 select_bitcast_fusion
  126.9 0.1 copy.27
  126.9 0.0 copy-start.1
  126.9 3.2 %top_k.9 = (f32[56,128]{1,0:T(8,128)}, s32[56,128]{1,0:T(8,128)}) sort(f32[56,128]{1,0:T(8,128)S(1)} %copy.27, s32[56,128]{1,0:T(8,128)S(1)} %iota.22), dimensions={1}, to_apply=%region_6.7 | sort | flops 93184 | bytes 114688 | tf_op jit(solution)/shard_map/top_k | solution.py:60
  130.1 0.0 copy-done.1
  (12 shorter events, 0.1 us)
Async XLA Ops:
  7.2 28.5 %copy-start = (s32[128]{0:T(128)S(1)}, s32[128]{0:T(128)}, u32[]{:S(2)}) copy-start(s32[128]{0:T(128)} %param.8) | copy-start | bytes 1540
  7.2 73.5 %all-gather.2.cloned.1.call-start = ((), (), s32[]{:S(2)}) async-start(), calls=%async_computation.2 | async-start | bytes 7798784 | tf_op jit(solution)/shard_map/all_gather | solution.py:47
  10.3 13.8 %all-to-all-start = ((s32[16,1,12]{2,1,0:T(1,128)}), s32[16,1,12]{2,1,0:T(1,128)S(1)}, u32[]{:S(2)}, u32[]{:S(2)}) async-start(s32[16,1,12]{2,1,0:T(1,128)} %bitcast.12), calls=%async_computation | async-start | bytes 16384 | tf_op jit(solution)/shard_map/all_to_all | solution.py:42
  114.5 10.2 %all-to-all-start.1 = ((f32[16,1,672]{2,1,0:T(1,128)}), f32[16,1,672]{2,1,0:T(1,128)S(1)}, u32[]{:S(2)}, u32[]{:S(2)}) async-start(f32[16,1,672]{2,1,0:T(1,128)} %reshape.217), calls=%async_computation.1 | async-start | bytes 98304 | tf_op jit(solution)/shard_map/all_to_all | solution.py:57
  126.9 3.2 %copy-start.1 = (f32[56,128]{1,0:T(8,128)}, f32[56,128]{1,0:T(8,128)S(1)}, u32[]{:S(2)}) copy-start(f32[56,128]{1,0:T(8,128)S(1)} %copy.27) | copy-start | bytes 86020
Sparse Core Ops, SparseCore 0:
  10.3 70.3 all-gather.1
where the time goes:
time: 137 us
  waiting for transfers between devices  49.2 us (36%)
  matrix products  28.8 us (21%)
  local copies, waits for them, and re-layouts  18.4 us (13%)
  other arithmetic  15.3 us (11%)
  between operations  14.2 us (10%)
  starting transfers between devices  10.9 us (8%)
    all_gather x1, waiting for transfers between devices, local(): piece = lax.all_gather(stacked, 'corpus', axis=0, tiled=True)  36.8 us
    dot_general x2, matrix products, maxsim_many(): jnp.einsum('srd,sgpd->srgp', query_sets, tile_sets, preferred_element_typ...  28.8 us
    gather x2, local copies, waits for them, and re-layouts, local(): chosen = fill_rows(passages[picked], lengths[picked])  11.7 us
    all_to_all x1, starting transfers between devices, local(): lax.all_to_all(wanted, 'corpus', split_axis=0, concat_axis=0, tiled=True)  7.41 us
    all_to_all x1, waiting for transfers between devices, local(): lax.all_to_all(fresh_scores, 'corpus', split_axis=0, concat_axis=0, tiled...  6.72 us
    select_n x1, other arithmetic, fill_rows(): return jnp.where(inside[:, :, None], tile_set, tile_set[:, :1, :])  6.55 us
    all_to_all x1, waiting for transfers between devices, local(): lax.all_to_all(wanted, 'corpus', split_axis=0, concat_axis=0, tiled=True)  5.01 us
    all_to_all x1, starting transfers between devices, local(): lax.all_to_all(fresh_scores, 'corpus', split_axis=0, concat_axis=0, tiled...  3.5 us
  transfers between devices with their start and end apart: 3, of which 3 were waited for; matrix products, arithmetic and copies ran while one was open for 17% of the time, Pallas kernels for 0%

commit v1 on v0

--- a/solution.py
+++ b/solution.py
@@ -44,7 +44,19 @@
     chosen = fill_rows(passages[picked], lengths[picked])
     by_scorer = chosen.reshape(peers, capacity, tile_rows, feature)
     stacked = queries.reshape(1, per_device * query_tok, feature)
-    piece = lax.all_gather(stacked, "corpus", axis=0, tiled=True)
+    lanes = lax.axis_size("corpus")
+    idx = 0
+    in_order = [stacked]
+    while idx < lanes - 1:
+        part_now = lax.ppermute(
+            in_order[-1],
+            axis_name="corpus",
+            perm=[(to_i, (to_i + 1) % lanes) for to_i in range(lanes)],
+        )
+        in_order.append(part_now)
+        idx += 1
+    local_now = jnp.concatenate(in_order[::-1], 0)
+    piece = jnp.roll(local_now, (lax.axis_index("corpus") + 1) * stacked.shape[0], 0)
     shards_here = piece.shape[0]
     group_size = math.gcd(shards_here, 8)
     turns = shards_here // group_size

time: 137 us -> 257 us (1.88)
  waiting for transfers between devices: 49.2 us -> 142 us
  local copies, waits for them, and re-layouts: 18.4 us -> 59.2 us
  between operations: 14.2 us -> 0.94 us
    ppermute x0 -> x15, waiting for transfers between devices: none -> 130 us  [local(): lax.ppermute(in_order[-1], axis_name='corpus', perm=[(to_i, (to_i + 1) %...]
    all_gather x1 -> x0, waiting for transfers between devices: 36.8 us -> none  [local(): piece = lax.all_gather(stacked, 'corpus', axis=0, tiled=True)]
    unnamed x7 -> x66, local copies, waits for them, and re-layouts: 0.95 us -> 34.1 us
    dynamic_slice x0 -> x1, local copies, waits for them, and re-layouts: none -> 6.73 us  [local(): jnp.roll(local_now, (lax.axis_index('corpus') + 1) * stacked.shape[0], 0)]
  transfers between devices with their start and end apart: 3 -> 17, of which waited for: 3 -> 15; matrix products, arithmetic and copies ran while one was open for 17% -> 9% of each run, Pallas kernels for 0% -> 0%
where the time goes in v1:
time: 257 us
  waiting for transfers between devices  142 us (55%)
  local copies, waits for them, and re-layouts  59.2 us (23%)
  matrix products  28.8 us (11%)
  other arithmetic  14.5 us (6%)
  starting transfers between devices  10.8 us (4%)
    ppermute x15, waiting for transfers between devices, local(): lax.ppermute(in_order[-1], axis_name='corpus', perm=[(to_i, (to_i + 1) %...  130 us
    unnamed x66, local copies, waits for them, and re-layouts  34.1 us
    dot_general x2, matrix products, maxsim_many(): jnp.einsum('srd,sgpd->srgp', query_sets, tile_sets, preferred_element_typ...  28.8 us
    gather x2, local copies, waits for them, and re-layouts, local(): chosen = fill_rows(passages[picked], lengths[picked])  11.8 us
    dynamic_slice x1, local copies, waits for them, and re-layouts, local(): jnp.roll(local_now, (lax.axis_index('corpus') + 1) * stacked.shape[0], 0)  6.73 us
    all_to_all x1, waiting for transfers between devices, local(): lax.all_to_all(fresh_scores, 'corpus', split_axis=0, concat_axis=0, tiled...  6.7 us
    select_n x1, other arithmetic, fill_rows(): return jnp.where(inside[:, :, None], tile_set, tile_set[:, :1, :])  6.51 us
    all_to_all x1, starting transfers between devices, local(): lax.all_to_all(wanted, 'corpus', split_axis=0, concat_axis=0, tiled=True)  5.82 us
  transfers between devices with their start and end apart: 17, of which 15 were waited for; matrix products, arithmetic and copies ran while one was open for 9% of the time, Pallas kernels for 0%

profile of v1, /device:TPU:0, one launch (start us, length us, event | category | flops | bytes accessed | tf_op | source)
XLA Modules:
  0.0 256.9 jit_solution(14145084762843627252)
XLA Ops:
  1.2 11.4 %collective-permute-done = bf16[1,1792,128]{2,1,0:T(8,128)(2,1)S(1)} collective-permute-done((bf16[1,1792,128]{2,1,0:T(8,128)(2,1)}, bf16[1,1792,128]{2,1,0:T(8,128)(2,1)S(1)}, u32[]{:S(2)}, u32[]{:S(2)}) %collective-permute-start) | collective-permute-done | bytes 458784 | tf_op jit(solution)/shard_map/ppermute | solution.py:51
  12.6 10.6 %collective-permute-done.1 = bf16[1,1792,128]{2,1,0:T(8,128)(2,1)S(1)} collective-permute-done((bf16[1,1792,128]{2,1,0:T(8,128)(2,1)S(1)}, bf16[1,1792,128]{2,1,0:T(8,128)(2,1)S(1)}, u32[]{:S(2)}, u32[]{:S(2)}) %collective-permute-start.1) | collective-permute-done | bytes 458784 | tf_op jit(solution)/shard_map/ppermute | solution.py:51
  23.2 10.6 %collective-permute-done.2 = bf16[1,1792,128]{2,1,0:T(8,128)(2,1)S(1)} collective-permute-done((bf16[1,1792,128]{2,1,0:T(8,128)(2,1)S(1)}, bf16[1,1792,128]{2,1,0:T(8,128)(2,1)S(1)}, u32[]{:S(2)}, u32[]{:S(2)}) %collective-permute-start.2) | collective-permute-done | bytes 458784 | tf_op jit(solution)/shard_map/ppermute | solution.py:51
  33.8 10.6 %collective-permute-done.3 = bf16[1,1792,128]{2,1,0:T(8,128)(2,1)S(1)} collective-permute-done((bf16[1,1792,128]{2,1,0:T(8,128)(2,1)S(1)}, bf16[1,1792,128]{2,1,0:T(8,128)(2,1)S(1)}, u32[]{:S(2)}, u32[]{:S(2)}) %collective-permute-start.3) | collective-permute-done | bytes 458784 | tf_op jit(solution)/shard_map/ppermute | solution.py:51
  44.4 10.6 %collective-permute-done.4 = bf16[1,1792,128]{2,1,0:T(8,128)(2,1)S(1)} collective-permute-done((bf16[1,1792,128]{2,1,0:T(8,128)(2,1)S(1)}, bf16[1,1792,128]{2,1,0:T(8,128)(2,1)S(1)}, u32[]{:S(2)}, u32[]{:S(2)}) %collective-permute-start.4) | collective-permute-done | bytes 458784 | tf_op jit(solution)/shard_map/ppermute | solution.py:51
  55.0 10.6 %collective-permute-done.5 = bf16[1,1792,128]{2,1,0:T(8,128)(2,1)S(1)} collective-permute-done((bf16[1,1792,128]{2,1,0:T(8,128)(2,1)S(1)}, bf16[1,1792,128]{2,1,0:T(8,128)(2,1)S(1)}, u32[]{:S(2)}, u32[]{:S(2)}) %collective-permute-start.5) | collective-permute-done | bytes 458784 | tf_op jit(solution)/shard_map/ppermute | solution.py:51
  65.6 10.6 %collective-permute-done.6 = bf16[1,1792,128]{2,1,0:T(8,128)(2,1)S(1)} collective-permute-done((bf16[1,1792,128]{2,1,0:T(8,128)(2,1)S(1)}, bf16[1,1792,128]{2,1,0:T(8,128)(2,1)S(1)}, u32[]{:S(2)}, u32[]{:S(2)}) %collective-permute-start.6) | collective-permute-done | bytes 458784 | tf_op jit(solution)/shard_map/ppermute | solution.py:51
  77.0 10.6 %collective-permute-done.7 = bf16[1,1792,128]{2,1,0:T(8,128)(2,1)S(1)} collective-permute-done((bf16[1,1792,128]{2,1,0:T(8,128)(2,1)S(1)}, bf16[1,1792,128]{2,1,0:T(8,128)(2,1)S(1)}, u32[]{:S(2)}, u32[]{:S(2)}) %collective-permute-start.7) | collective-permute-done | bytes 458784 | tf_op jit(solution)/shard_map/ppermute | solution.py:51
  88.3 10.6 %collective-permute-done.8 = bf16[1,1792,128]{2,1,0:T(8,128)(2,1)S(1)} collective-permute-done((bf16[1,1792,128]{2,1,0:T(8,128)(2,1)S(1)}, bf16[1,1792,128]{2,1,0:T(8,128)(2,1)S(1)}, u32[]{:S(2)}, u32[]{:S(2)}) %collective-permute-start.8) | collective-permute-done | bytes 458784 | tf_op jit(solution)/shard_map/ppermute | solution.py:51
  99.7 10.6 %collective-permute-done.9 = bf16[1,1792,128]{2,1,0:T(8,128)(2,1)S(1)} collective-permute-done((bf16[1,1792,128]{2,1,0:T(8,128)(2,1)S(1)}, bf16[1,1792,128]{2,1,0:T(8,128)(2,1)S(1)}, u32[]{:S(2)}, u32[]{:S(2)}) %collective-permute-start.9) | collective-permute-done | bytes 458784 | tf_op jit(solution)/shard_map/ppermute | solution.py:51
  111.1 10.6 %collective-permute-done.10 = bf16[1,1792,128]{2,1,0:T(8,128)(2,1)S(1)} collective-permute-done((bf16[1,1792,128]{2,1,0:T(8,128)(2,1)S(1)}, bf16[1,1792,128]{2,1,0:T(8,128)(2,1)S(1)}, u32[]{:S(2)}, u32[]{:S(2)}) %collective-permute-start.10) | collective-permute-done | bytes 458784 | tf_op jit(solution)/shard_map/ppermute | solution.py:51
  124.0 9.1 %collective-permute-done.11 = bf16[1,1792,128]{2,1,0:T(8,128)(2,1)S(1)} collective-permute-done((bf16[1,1792,128]{2,1,0:T(8,128)(2,1)S(1)}, bf16[1,1792,128]{2,1,0:T(8,128)(2,1)S(1)}, u32[]{:S(2)}, u32[]{:S(2)}) %collective-permute-start.11) | collective-permute-done | bytes 458784 | tf_op jit(solution)/shard_map/ppermute | solution.py:51
  133.9 5.8 %all-to-all-start = ((s32[16,1,12]{2,1,0:T(1,128)}), s32[16,1,12]{2,1,0:T(1,128)S(1)}, u32[]{:S(2)}, u32[]{:S(2)}) async-start(s32[16,1,12]{2,1,0:T(1,128)} %bitcast.12), calls=%async_computation | async-start | bytes 16384 | tf_op jit(solution)/shard_map/all_to_all | solution.py:42
  140.4 5.7 %all-to-all-done = s32[16,1,12]{2,1,0:T(1,128)S(1)} async-done(((s32[16,1,12]{2,1,0:T(1,128)}), s32[16,1,12]{2,1,0:T(1,128)S(1)}, u32[]{:S(2)}, u32[]{:S(2)}) %all-to-all-start) | async-done | bytes 800 | tf_op jit(solution)/shard_map/all_to_all | solution.py:42
  146.3 10.2 %gather_fusion.1 = bf16[192,128,128]{2,1,0:T(8,128)(2,1)} fusion(bf16[128,128,128]{2,1,0:T(8,128)(2,1)} %param.7, s32[1024]{0:T(1024)S(1)} %get-tuple-element.49), kind=kCustom, calls=%fused_computation.1 | custom fusion | bytes 12583680 | tf_op jit(solution)/shard_map/gather | solution.py:44
  156.5 1.3 slice_reduce_fusion
  157.9 1.6 gather_fusion
  159.7 0.9 collective-permute-start.14
  160.5 6.5 %broadcast_select_fusion = bf16[2,8,12,128,128]{4,3,2,1,0:T(8,128)(2,1)} fusion(bf16[2,8,12,128,128]{4,3,2,1,0:T(8,128)(2,1)} %bitcast.77, pred[2,8,12,128]{3,2,1,0:T(8,128)(4,1)S(1)} %iota_compare_fusion, bf16[2,8,12,128]{3,2,1,0:T(8,128)(2,1)S(1)} %broadcast_in_dim.64), kind=kLoop, calls=%fused_computation.10 | loop fusion | flops 3145728 | bytes 12656640 | tf_op jit(solution)/shard_map/jit(_where)/select_n | solution.py:24
  167.1 3.7 %collective-permute-done.14 = bf16[1,1792,128]{2,1,0:T(8,128)(2,1)S(1)} collective-permute-done((bf16[1,1792,128]{2,1,0:T(8,128)(2,1)}, bf16[1,1792,128]{2,1,0:T(8,128)(2,1)S(1)}, u32[]{:S(2)}, u32[]{:S(2)}) %collective-permute-start.14) | collective-permute-done | bytes 458784 | tf_op jit(solution)/shard_map/ppermute | solution.py:51
  171.5 1.8 constant_dynamic-update-slice_fusion.30
  173.4 1.8 constant_dynamic-update-slice_fusion.29
  175.2 0.8 constant_dynamic-update-slice_fusion.28
  176.0 0.8 constant_dynamic-update-slice_fusion.27
  177.6 0.8 constant_dynamic-update-slice_fusion.25
  179.3 0.8 constant_dynamic-update-slice_fusion.23
  181.7 0.8 constant_dynamic-update-slice_fusion.20
  182.5 0.8 constant_dynamic-update-slice_fusion.19
  184.1 0.8 constant_dynamic-update-slice_fusion.17
  184.9 0.8 constant_dynamic-update-slice_fusion.16
  186.5 1.8 constant_dynamic-update-slice_fusion.14
  188.3 1.9 constant_dynamic-update-slice_fusion.13
  190.2 0.8 constant_dynamic-update-slice_fusion.12
  191.1 0.8 constant_dynamic-update-slice_fusion.11
  193.5 0.8 constant_dynamic-update-slice_fusion.8
  194.3 0.8 constant_dynamic-update-slice_fusion.7
  195.1 0.8 constant_dynamic-update-slice_fusion.6
  197.5 0.8 constant_dynamic-update-slice_fusion.3
  198.3 0.8 constant_dynamic-update-slice_fusion.2
  200.8 6.7 %constant_dynamic-slice_fusion = bf16[16,1792,128]{2,1,0:T(8,128)(2,1)} fusion(bf16[32,1792,128]{2,1,0:T(8,128)(2,1)} %constant_dynamic-update-slice_fusion, s32[]{:T(128)S(6)} %select_n.71), kind=kLoop, calls=%fused_computation.76 | loop fusion | bytes 14680068 | tf_op jit(solution)/shard_map/jit(_roll_dynamic)/dynamic_slice | solution.py:59
  207.5 32.9 %while.10 = (s32[]{:T(128)}, f32[2,8,56,12]{2,1,0,3:T(8,128)S(1)}, bf16[2,8,1792,128]{3,2,1,0:T(8,128)(2,1)}, bf16[2,8,12,128,128]{4,3,2,1,0:T(8,128)(2,1)}, s32[]{:T(128)}, /*index=5*/f32[]{:T(128)}) while((s32[]{:T(128)}, f32[2,8,56,12]{2,1,0,3:T(8,128)S(1)}, bf16[2,8,1792,128]{3,2,1,0:T(8,128)(2,1)}, ...), condition=%wide.region_5.6_spmd, body=%wide.region_2.5_spmd.sunk | while | flops 5659164672 | bytes 11065421 | solution.py:65
  207.5 14.4 %convolution_reduce_fusion.2 = f32[8,1792,12]{1,2,0:T(8,128)S(1)} fusion(bf16[2,8,1792,128]{3,2,1,0:T(8,128)(2,1)} %get-tuple-element.89, s32[]{:T(128)} %get-tuple-element.81, bf16[2,8,12,128,128]{4,3,2,1,0:T(8,128)(2,1)} %get-tuple-element.90), kind=kOutput, calls=%fused_computation.3.clone.1 | convolution fusion | flops 5658992640 | bytes 7504896 | tf_op jit(solution)/shard_map/while/body/eval_jaxpr/srd,sgpd->srgp/dot_general | solution.py:11
  222.3 0.8 reshape.220
  224.0 14.4 %convolution_reduce_fusion.2 = f32[8,1792,12]{1,2,0:T(8,128)S(1)} fusion(bf16[2,8,1792,128]{3,2,1,0:T(8,128)(2,1)} %get-tuple-element.89, s32[]{:T(128)} %get-tuple-element.81, bf16[2,8,12,128,128]{4,3,2,1,0:T(8,128)(2,1)} %get-tuple-element.90), kind=kOutput, calls=%fused_computation.3.clone.1 | convolution fusion | flops 5658992640 | bytes 7504896 | tf_op jit(solution)/shard_map/while/body/eval_jaxpr/srd,sgpd->srgp/dot_general | solution.py:11
  238.8 0.8 reshape.220
  241.2 3.5 %all-to-all-start.1 = ((f32[16,1,672]{2,1,0:T(1,128)}), f32[16,1,672]{2,1,0:T(1,128)S(1)}, u32[]{:S(2)}, u32[]{:S(2)}) async-start(f32[16,1,672]{2,1,0:T(1,128)} %reshape.217), calls=%async_computation.1 | async-start | bytes 98304 | tf_op jit(solution)/shard_map/all_to_all | solution.py:69
  244.8 6.7 %all-to-all-done.1 = f32[16,1,672]{2,1,0:T(1,128)S(1)} async-done(((f32[16,1,672]{2,1,0:T(1,128)}), f32[16,1,672]{2,1,0:T(1,128)S(1)}, u32[]{:S(2)}, u32[]{:S(2)}) %all-to-all-start.1) | async-done | bytes 43040 | tf_op jit(solution)/shard_map/all_to_all | solution.py:69
  253.7 3.2 %top_k.9 = (f32[56,128]{1,0:T(8,128)}, s32[56,128]{1,0:T(8,128)}) sort(f32[56,128]{1,0:T(8,128)S(1)} %copy.27, s32[56,128]{1,0:T(8,128)S(1)} %iota.22), dimensions={1}, to_apply=%region_6.7 | sort | flops 93184 | bytes 114688 | tf_op jit(solution)/shard_map/top_k | solution.py:72
  (93 shorter events, 23.6 us)
Async XLA Ops:
  0.6 157.2 %copy-start = (s32[128]{0:T(128)S(1)}, s32[128]{0:T(128)}, u32[]{:S(2)}) copy-start(s32[128]{0:T(128)} %param.8) | copy-start | bytes 1540
  0.6 11.9 %collective-permute-start = (bf16[1,1792,128]{2,1,0:T(8,128)(2,1)}, bf16[1,1792,128]{2,1,0:T(8,128)(2,1)S(1)}, u32[]{:S(2)}, u32[]{:S(2)}) collective-permute-start(bf16[1,1792,128]{2,1,0:T(8,128)(2,1)} %bitcast.79), channel_id=1, source_target_pairs={{0,1},{1,2},{2,3},{3,4},{4,5},{5,6},{6,7},{7,8},{8,9},{9,10},{10,1... | collective-permute-start | bytes 1376264 | tf_op jit(solution)/shard_map/ppermute | solution.py:51
  12.5 10.6 %collective-permute-start.1 = (bf16[1,1792,128]{2,1,0:T(8,128)(2,1)S(1)}, bf16[1,1792,128]{2,1,0:T(8,128)(2,1)S(1)}, u32[]{:S(2)}, u32[]{:S(2)}) collective-permute-start(bf16[1,1792,128]{2,1,0:T(8,128)(2,1)S(1)} %collective-permute-done), channel_id=1, source_target_pairs={{0,1},{1,2},{2,3},{3,4},{4,5},{5,6},{6,7},{7,8},{8,9},{9,10},{10,1... | collective-permute-start | bytes 1376264 | tf_op jit(solution)/shard_map/ppermute | solution.py:51
  23.1 10.6 %collective-permute-start.2 = (bf16[1,1792,128]{2,1,0:T(8,128)(2,1)S(1)}, bf16[1,1792,128]{2,1,0:T(8,128)(2,1)S(1)}, u32[]{:S(2)}, u32[]{:S(2)}) collective-permute-start(bf16[1,1792,128]{2,1,0:T(8,128)(2,1)S(1)} %collective-permute-done.1), channel_id=1, source_target_pairs={{0,1},{1,2},{2,3},{3,4},{4,5},{5,6},{6,7},{7,8},{8,9},{9,10},{10,1... | collective-permute-start | bytes 1376264 | tf_op jit(solution)/shard_map/ppermute | solution.py:51
  33.8 10.6 %collective-permute-start.3 = (bf16[1,1792,128]{2,1,0:T(8,128)(2,1)S(1)}, bf16[1,1792,128]{2,1,0:T(8,128)(2,1)S(1)}, u32[]{:S(2)}, u32[]{:S(2)}) collective-permute-start(bf16[1,1792,128]{2,1,0:T(8,128)(2,1)S(1)} %collective-permute-done.2), channel_id=1, source_target_pairs={{0,1},{1,2},{2,3},{3,4},{4,5},{5,6},{6,7},{7,8},{8,9},{9,10},{10,1... | collective-permute-start | bytes 1376264 | tf_op jit(solution)/shard_map/ppermute | solution.py:51
  44.4 10.6 %collective-permute-start.4 = (bf16[1,1792,128]{2,1,0:T(8,128)(2,1)S(1)}, bf16[1,1792,128]{2,1,0:T(8,128)(2,1)S(1)}, u32[]{:S(2)}, u32[]{:S(2)}) collective-permute-start(bf16[1,1792,128]{2,1,0:T(8,128)(2,1)S(1)} %collective-permute-done.3), channel_id=1, source_target_pairs={{0,1},{1,2},{2,3},{3,4},{4,5},{5,6},{6,7},{7,8},{8,9},{9,10},{10,1... | collective-permute-start | bytes 1376264 | tf_op jit(solution)/shard_map/ppermute | solution.py:51
  55.0 10.6 %collective-permute-start.5 = (bf16[1,1792,128]{2,1,0:T(8,128)(2,1)S(1)}, bf16[1,1792,128]{2,1,0:T(8,128)(2,1)S(1)}, u32[]{:S(2)}, u32[]{:S(2)}) collective-permute-start(bf16[1,1792,128]{2,1,0:T(8,128)(2,1)S(1)} %collective-permute-done.4), channel_id=1, source_target_pairs={{0,1},{1,2},{2,3},{3,4},{4,5},{5,6},{6,7},{7,8},{8,9},{9,10},{10,1... | collective-permute-start | bytes 1376264 | tf_op jit(solution)/shard_map/ppermute | solution.py:51
  65.6 10.6 %collective-permute-start.6 = (bf16[1,1792,128]{2,1,0:T(8,128)(2,1)S(1)}, bf16[1,1792,128]{2,1,0:T(8,128)(2,1)S(1)}, u32[]{:S(2)}, u32[]{:S(2)}) collective-permute-start(bf16[1,1792,128]{2,1,0:T(8,128)(2,1)S(1)} %collective-permute-done.5), channel_id=1, source_target_pairs={{0,1},{1,2},{2,3},{3,4},{4,5},{5,6},{6,7},{7,8},{8,9},{9,10},{10,1... | collective-permute-start | bytes 1376264 | tf_op jit(solution)/shard_map/ppermute | solution.py:51
  76.2 0.8 copy-start.2
  77.0 10.6 %collective-permute-start.7 = (bf16[1,1792,128]{2,1,0:T(8,128)(2,1)S(1)}, bf16[1,1792,128]{2,1,0:T(8,128)(2,1)S(1)}, u32[]{:S(2)}, u32[]{:S(2)}) collective-permute-start(bf16[1,1792,128]{2,1,0:T(8,128)(2,1)S(1)} %collective-permute-done.6), channel_id=1, source_target_pairs={{0,1},{1,2},{2,3},{3,4},{4,5},{5,6},{6,7},{7,8},{8,9},{9,10},{10,1... | collective-permute-start | bytes 1376264 | tf_op jit(solution)/shard_map/ppermute | solution.py:51
  87.6 0.8 copy-start.4
  88.3 10.6 %collective-permute-start.8 = (bf16[1,1792,128]{2,1,0:T(8,128)(2,1)S(1)}, bf16[1,1792,128]{2,1,0:T(8,128)(2,1)S(1)}, u32[]{:S(2)}, u32[]{:S(2)}) collective-permute-start(bf16[1,1792,128]{2,1,0:T(8,128)(2,1)S(1)} %collective-permute-done.7), channel_id=1, source_target_pairs={{0,1},{1,2},{2,3},{3,4},{4,5},{5,6},{6,7},{7,8},{8,9},{9,10},{10,1... | collective-permute-start | bytes 1376264 | tf_op jit(solution)/shard_map/ppermute | solution.py:51
  98.9 0.8 copy-start.6
  99.7 10.6 %collective-permute-start.9 = (bf16[1,1792,128]{2,1,0:T(8,128)(2,1)S(1)}, bf16[1,1792,128]{2,1,0:T(8,128)(2,1)S(1)}, u32[]{:S(2)}, u32[]{:S(2)}) collective-permute-start(bf16[1,1792,128]{2,1,0:T(8,128)(2,1)S(1)} %collective-permute-done.8), channel_id=1, source_target_pairs={{0,1},{1,2},{2,3},{3,4},{4,5},{5,6},{6,7},{7,8},{8,9},{9,10},{10,1... | collective-permute-start | bytes 1376264 | tf_op jit(solution)/shard_map/ppermute | solution.py:51
  110.3 0.8 copy-start.8
  111.1 10.6 %collective-permute-start.10 = (bf16[1,1792,128]{2,1,0:T(8,128)(2,1)S(1)}, bf16[1,1792,128]{2,1,0:T(8,128)(2,1)S(1)}, u32[]{:S(2)}, u32[]{:S(2)}) collective-permute-start(bf16[1,1792,128]{2,1,0:T(8,128)(2,1)S(1)} %collective-permute-done.9), channel_id=1, source_target_pairs={{0,1},{1,2},{2,3},{3,4},{4,5},{5,6},{6,7},{7,8},{8,9},{9,10},{10,1... | collective-permute-start | bytes 1376264 | tf_op jit(solution)/shard_map/ppermute | solution.py:51
  121.7 0.8 copy-start.10
  122.5 10.6 %collective-permute-start.11 = (bf16[1,1792,128]{2,1,0:T(8,128)(2,1)S(1)}, bf16[1,1792,128]{2,1,0:T(8,128)(2,1)S(1)}, u32[]{:S(2)}, u32[]{:S(2)}) collective-permute-start(bf16[1,1792,128]{2,1,0:T(8,128)(2,1)S(1)} %collective-permute-done.10), channel_id=1, source_target_pairs={{0,1},{1,2},{2,3},{3,4},{4,5},{5,6},{6,7},{7,8},{8,9},{9,10},{10,1... | collective-permute-start | bytes 1376264 | tf_op jit(solution)/shard_map/ppermute | solution.py:51
  133.1 13.2 %copy-start.12 = (bf16[1,1792,128]{2,1,0:T(8,128)(2,1)}, bf16[1,1792,128]{2,1,0:T(8,128)(2,1)S(1)}, u32[]{:S(2)}) copy-start(bf16[1,1792,128]{2,1,0:T(8,128)(2,1)S(1)} %collective-permute-done.11) | copy-start | bytes 1376260
  133.1 13.1 %collective-permute-start.12 = (bf16[1,1792,128]{2,1,0:T(8,128)(2,1)S(1)}, bf16[1,1792,128]{2,1,0:T(8,128)(2,1)}, u32[]{:S(2)}, u32[]{:S(2)}) collective-permute-start(bf16[1,1792,128]{2,1,0:T(8,128)(2,1)S(1)} %collective-permute-done.11), channel_id=1, source_target_pairs={{0,1},{1,2},{2,3},{3,4},{4,5},{5,6},{6,7},{7,8},{8,9},{9,10},{10,1... | collective-permute-start | bytes 1376264 | tf_op jit(solution)/shard_map/ppermute | solution.py:51
  133.9 12.2 %all-to-all-start = ((s32[16,1,12]{2,1,0:T(1,128)}), s32[16,1,12]{2,1,0:T(1,128)S(1)}, u32[]{:S(2)}, u32[]{:S(2)}) async-start(s32[16,1,12]{2,1,0:T(1,128)} %bitcast.12), calls=%async_computation | async-start | bytes 16384 | tf_op jit(solution)/shard_map/all_to_all | solution.py:42
  146.2 13.5 %collective-permute-start.13 = (bf16[1,1792,128]{2,1,0:T(8,128)(2,1)}, bf16[1,1792,128]{2,1,0:T(8,128)(2,1)}, u32[]{:S(2)}, u32[]{:S(2)}) collective-permute-start(bf16[1,1792,128]{2,1,0:T(8,128)(2,1)} %collective-permute-done.12), channel_id=1, source_target_pairs={{0,1},{1,2},{2,3},{3,4},{4,5},{5,6},{6,7},{7,8},{8,9},{9,10},{10,1... | collective-permute-start | bytes 1376264 | tf_op jit(solution)/shard_map/ppermute | solution.py:51
  156.5 28.4 %copy-start.1 = (bf16[56,32,128]{2,1,0:T(8,128)(2,1)S(1)}, bf16[56,32,128]{2,1,0:T(8,128)(2,1)}, u32[]{:S(2)}) copy-start(bf16[56,32,128]{2,1,0:T(8,128)(2,1)} %param.6) | copy-start | bytes 1376260
  159.5 15.7 %copy-start.13 = (bf16[1,1792,128]{2,1,0:T(8,128)(2,1)S(1)}, bf16[1,1792,128]{2,1,0:T(8,128)(2,1)}, u32[]{:S(2)}) copy-start(bf16[1,1792,128]{2,1,0:T(8,128)(2,1)} %copy-done.12) | copy-start | bytes 1376260
  159.5 16.5 %copy-start.11 = (bf16[1,1792,128]{2,1,0:T(8,128)(2,1)S(1)}, bf16[1,1792,128]{2,1,0:T(8,128)(2,1)}, u32[]{:S(2)}) copy-start(bf16[1,1792,128]{2,1,0:T(8,128)(2,1)} %copy-done.10) | copy-start | bytes 1376260
  159.5 17.3 %copy-start.9 = (bf16[1,1792,128]{2,1,0:T(8,128)(2,1)S(1)}, bf16[1,1792,128]{2,1,0:T(8,128)(2,1)}, u32[]{:S(2)}) copy-start(bf16[1,1792,128]{2,1,0:T(8,128)(2,1)} %copy-done.8) | copy-start | bytes 1376260
  159.5 18.1 %copy-start.7 = (bf16[1,1792,128]{2,1,0:T(8,128)(2,1)S(1)}, bf16[1,1792,128]{2,1,0:T(8,128)(2,1)}, u32[]{:S(2)}) copy-start(bf16[1,1792,128]{2,1,0:T(8,128)(2,1)} %copy-done.6) | copy-start | bytes 1376260
  159.5 18.9 %copy-start.5 = (bf16[1,1792,128]{2,1,0:T(8,128)(2,1)S(1)}, bf16[1,1792,128]{2,1,0:T(8,128)(2,1)}, u32[]{:S(2)}) copy-start(bf16[1,1792,128]{2,1,0:T(8,128)(2,1)} %copy-done.4) | copy-start | bytes 1376260
  159.5 19.7 %copy-start.3 = (bf16[1,1792,128]{2,1,0:T(8,128)(2,1)S(1)}, bf16[1,1792,128]{2,1,0:T(8,128)(2,1)}, u32[]{:S(2)}) copy-start(bf16[1,1792,128]{2,1,0:T(8,128)(2,1)} %copy-done.2) | copy-start | bytes 1376260
  159.7 11.1 %collective-permute-start.14 = (bf16[1,1792,128]{2,1,0:T(8,128)(2,1)}, bf16[1,1792,128]{2,1,0:T(8,128)(2,1)S(1)}, u32[]{:S(2)}, u32[]{:S(2)}) collective-permute-start(bf16[1,1792,128]{2,1,0:T(8,128)(2,1)} %collective-permute-done.13), channel_id=1, source_target_pairs={{0,1},{1,2},{2,3},{3,4},{4,5},{5,6},{6,7},{7,8},{8,9},{9,10},{10,1... | collective-permute-start | bytes 1376264 | tf_op jit(solution)/shard_map/ppermute | solution.py:51
  207.5 37.3 %copy-start.15 = (s32[1,128]{1,0:T(1,128)S(1)}, s32[1,128]{1,0:T(1,128)}, u32[]{:S(2)}) copy-start(s32[1,128]{1,0:T(1,128)} %param.9) | copy-start | bytes 1540
  241.2 10.2 %all-to-all-start.1 = ((f32[16,1,672]{2,1,0:T(1,128)}), f32[16,1,672]{2,1,0:T(1,128)S(1)}, u32[]{:S(2)}, u32[]{:S(2)}) async-start(f32[16,1,672]{2,1,0:T(1,128)} %reshape.217), calls=%async_computation.1 | async-start | bytes 98304 | tf_op jit(solution)/shard_map/all_to_all | solution.py:69
  253.7 3.2 %copy-start.14 = (f32[56,128]{1,0:T(8,128)}, f32[56,128]{1,0:T(8,128)S(1)}, u32[]{:S(2)}) copy-start(f32[56,128]{1,0:T(8,128)S(1)} %copy.27) | copy-start | bytes 86020
